TPU v7x, 32 devices: a whole 2x2x4 slice. The times are simulated.
32 devices in a mesh: rep: 4 (over y, x), inner: 8 (over z, core).
Axes of the slice: x: 2, y: 2, z: 4, core: 2. Of those that a mesh axis runs over, the one named last changes fastest.
Arguments:
- tokens: bfloat16 [4096, 1024], P(('rep', 'inner')), may hold values from -6 to 6
- cotangent: bfloat16 [4096, 1024], P(('rep', 'inner')), may hold values from -6 to 6
- qkv_weight: bfloat16 [1024, 3072], P('inner'), may hold values from -0.1875 to 0.1875
- out_weight: bfloat16 [1024, 1024], P('inner'), may hold values from -3.5 to 3.5
- in_weight: bfloat16 [1024, 5248], P('inner'), may hold values from -0.1875 to 0.1875
- down_weight: bfloat16 [2624, 1024], P('inner'), may hold values from -0.125 to 0.125
- gain_one: bfloat16 [1024], P('inner'), may hold values from 0.5 to 1.5
- gain_two: bfloat16 [1024], P('inner'), may hold values from 0.5 to 1.5
Outputs:
- layer_out: bfloat16 [4096, 1024], P(('rep', 'inner'))
- input_grad: bfloat16 [4096, 1024], P(('rep', 'inner'))
- qkv_grad: float32 [1024, 3072], P('inner')
- out_grad: float32 [1024, 1024], P('inner')
- in_grad: float32 [1024, 5248], P('inner')
- down_grad: float32 [2624, 1024], P('inner')
- gain_one_grad: float32 [1024], P('inner')
- gain_two_grad: float32 [1024], P('inner')
All inputs are finite; a program needn't handle non-finite values.
Results may differ from a plain program's by a relative error of at most 0.023.
Values may be sent and summed in bfloat16 or wider, within the bound.
No kernel may reach another device: no remote copies, remote signals or barrier semaphores. Data moves between devices by JAX's collectives and lax.ppermute only.
A program may use at most 256 MiB of HBM per device.

v0:
```python
import jax
import jax.numpy as jnp
from jax import lax
from jax.sharding import PartitionSpec as P

HEAD_DIM = 64
EPSILON = 1e-05
THETA = 160000.0


def norm_rows(values, gain_row):
    centred = values - jnp.mean(values, axis=-1, keepdims=True)
    inv_scale = lax.rsqrt(jnp.mean(centred * centred, axis=-1, keepdims=True) + EPSILON)
    return centred * inv_scale * gain_row


def rotate(values, cos_table, sine_table):
    half_width = values.shape[-1] // 2
    first_half = values[..., :half_width]
    second_half = values[..., half_width:]
    return jnp.concatenate(
        [
            first_half * cos_table - second_half * sine_table,
            second_half * cos_table + first_half * sine_table,
        ],
        axis=-1,
    )


def geglu(hidden):
    half_width = hidden.shape[-1] // 2
    return jax.nn.gelu(hidden[:, :half_width], approximate=False) * hidden[:, half_width:]


def contract_rows(left_mat, right_mat):
    return lax.dot_general(
        left_mat, right_mat, (((0,), (0,)), ((), ())), preferred_element_type=jnp.float32
    )


def contract_cols(left_mat, right_mat):
    return lax.dot_general(
        left_mat, right_mat, (((1,), (1,)), ((), ())), preferred_element_type=jnp.float32
    )


def on_device(
    tokens, cotangent, qkv_weight, out_weight, in_weight, down_weight, gain_one, gain_two
):
    row_count = tokens.shape[0]
    model_width = tokens.shape[1]
    head_count = model_width // HEAD_DIM
    score_scale = HEAD_DIM ** (-0.5)
    gathered = (
        lax.all_gather(qkv_weight, "inner", axis=0, tiled=True),
        lax.all_gather(out_weight, "inner", axis=0, tiled=True),
        lax.all_gather(in_weight, "inner", axis=0, tiled=True),
        lax.all_gather(down_weight, "inner", axis=0, tiled=True),
        lax.all_gather(gain_one, "inner", axis=0, tiled=True),
        lax.all_gather(gain_two, "inner", axis=0, tiled=True),
    )
    w_qkv, w_out, w_in, w_down, first_gain, second_gain = gathered
    tok_place = (
        lax.axis_index("inner") * row_count + jnp.arange(row_count, dtype=jnp.int32)
    ).astype(jnp.float32)
    inv_freq = 1.0 / THETA ** (jnp.arange(HEAD_DIM // 2, dtype=jnp.float32) * (2.0 / HEAD_DIM))
    tok_angle = tok_place[:, None] * inv_freq[None, :]
    cos_table = jnp.cos(tok_angle)[:, None, :]
    sine_table = jnp.sin(tok_angle)[:, None, :]

    def split_heads(projected):
        query_part = rotate(
            projected[:, :model_width].reshape(row_count, head_count, HEAD_DIM),
            cos_table,
            sine_table,
        )
        key_part = rotate(
            projected[:, model_width : 2 * model_width].reshape(row_count, head_count, HEAD_DIM),
            cos_table,
            sine_table,
        )
        value_part = projected[:, 2 * model_width :].reshape(row_count, head_count, HEAD_DIM)
        return (query_part, key_part, value_part)

    inputs = tokens.astype(jnp.float32)
    gain_first = first_gain.astype(jnp.float32)
    gain_second = second_gain.astype(jnp.float32)
    normed_one = norm_rows(inputs, gain_first).astype(jnp.bfloat16)
    projected = jnp.dot(normed_one, w_qkv, preferred_element_type=jnp.float32)
    query_part, key_part, value_part = split_heads(projected)
    query_heads = query_part.astype(jnp.bfloat16)
    key_flat = key_part.reshape(row_count, model_width).astype(jnp.bfloat16)
    value_flat = value_part.reshape(row_count, model_width).astype(jnp.bfloat16)
    all_keys, all_values = (
        lax.all_gather(key_flat, "inner", axis=0, tiled=True),
        lax.all_gather(value_flat, "inner", axis=0, tiled=True),
    )
    key_count = all_keys.shape[0]
    block_count = max(1, key_count // 512)
    block_rows = key_count // block_count

    def split_blocks(flat):
        return flat.reshape(block_count, block_rows, head_count, HEAD_DIM)

    def scores_of(key_block):
        return (
            jnp.einsum("qhd,khd->hqk", query_heads, key_block, preferred_element_type=jnp.float32)
            * score_scale
        )

    def stats_step(stat_carry, key_block):
        row_top, row_mass = stat_carry
        scores = scores_of(key_block)
        new_top = jnp.maximum(row_top, jnp.max(scores, axis=-1))
        row_mass = row_mass * jnp.exp(row_top - new_top) + jnp.sum(
            jnp.exp(scores - new_top[..., None]), axis=-1
        )
        return ((new_top, row_mass), None)

    start_top = jnp.full((head_count, row_count), -jnp.inf, jnp.float32)
    start_mass = jnp.zeros((head_count, row_count), jnp.float32)
    stat_final, unused_out = lax.scan(stats_step, (start_top, start_mass), split_blocks(all_keys))
    log_mass = stat_final[0] + jnp.log(stat_final[1])

    def mix_step(total_mix, blocks_pair):
        key_block, value_block = blocks_pair
        weights = jnp.exp(scores_of(key_block) - log_mass[..., None]).astype(jnp.bfloat16)
        return (
            total_mix
            + jnp.einsum("hqk,khd->qhd", weights, value_block, preferred_element_type=jnp.float32),
            None,
        )

    start_mix = jnp.zeros((row_count, head_count, HEAD_DIM), jnp.float32)
    mixed_heads, unused_mix = lax.scan(
        mix_step, start_mix, (split_blocks(all_keys), split_blocks(all_values))
    )
    attended = mixed_heads.reshape(row_count, model_width).astype(jnp.bfloat16)
    middle = inputs + jnp.dot(attended, w_out, preferred_element_type=jnp.float32)
    normed_two = norm_rows(middle, gain_second).astype(jnp.bfloat16)
    hidden = jnp.dot(normed_two, w_in, preferred_element_type=jnp.float32)
    gated = geglu(hidden).astype(jnp.bfloat16)
    layer_out = middle + jnp.dot(gated, w_down, preferred_element_type=jnp.float32)
    again = (
        lax.all_gather(qkv_weight, "inner", axis=0, tiled=True),
        lax.all_gather(out_weight, "inner", axis=0, tiled=True),
        lax.all_gather(in_weight, "inner", axis=0, tiled=True),
        lax.all_gather(down_weight, "inner", axis=0, tiled=True),
        lax.all_gather(gain_one, "inner", axis=0, tiled=True),
        lax.all_gather(gain_two, "inner", axis=0, tiled=True),
    )
    w_qkv, w_out, w_in, w_down, first_gain, second_gain = again
    gain_first = first_gain.astype(jnp.float32)
    gain_second = second_gain.astype(jnp.float32)
    grad_down = contract_rows(gated, cotangent)
    grad_gated = contract_cols(cotangent, w_down)
    gate_value, pull_gate = jax.vjp(geglu, hidden)
    grad_hidden = pull_gate(grad_gated)[0].astype(jnp.bfloat16)
    grad_in = contract_rows(normed_two, grad_hidden)
    grad_normed_two = contract_cols(grad_hidden, w_in)
    norm_value, pull_two = jax.vjp(norm_rows, middle, gain_second)
    back_middle, grad_gain_two = pull_two(grad_normed_two)
    grad_middle = cotangent.astype(jnp.float32) + back_middle
    grad_branch = grad_middle.astype(jnp.bfloat16)
    grad_wout = contract_rows(attended, grad_branch)
    grad_attended = contract_cols(grad_branch, w_out).astype(jnp.bfloat16)
    grad_heads = grad_attended.reshape(row_count, head_count, HEAD_DIM)
    offset = jnp.sum(
        grad_heads.astype(jnp.float32)
        * attended.reshape(row_count, head_count, HEAD_DIM).astype(jnp.float32),
        axis=-1,
    ).T
    all_keys, all_values = (
        lax.all_gather(key_flat, "inner", axis=0, tiled=True),
        lax.all_gather(value_flat, "inner", axis=0, tiled=True),
    )

    def score_grads(key_block, value_block):
        soft_probs = jnp.exp(scores_of(key_block) - log_mass[..., None])
        grad_probs = jnp.einsum(
            "qhd,khd->hqk", grad_heads, value_block, preferred_element_type=jnp.float32
        )
        grad_scores = (soft_probs * (grad_probs - offset[..., None])).astype(jnp.bfloat16)
        return (soft_probs, grad_scores)

    def back_step(grad_query, blocks_pair):
        key_block, value_block = blocks_pair
        soft_probs, grad_scores = score_grads(key_block, value_block)
        grad_value = jnp.einsum(
            "hqk,qhd->khd",
            soft_probs.astype(jnp.bfloat16),
            grad_heads,
            preferred_element_type=jnp.float32,
        )
        grad_key = (
            jnp.einsum("hqk,qhd->khd", grad_scores, query_heads, preferred_element_type=jnp.float32)
            * score_scale
        )
        grad_query = (
            grad_query
            + jnp.einsum("hqk,khd->qhd", grad_scores, key_block, preferred_element_type=jnp.float32)
            * score_scale
        )
        return (grad_query, (grad_key, grad_value))

    start_query = jnp.zeros((row_count, head_count, HEAD_DIM), jnp.float32)
    grad_query, key_parts = lax.scan(
        back_step, start_query, (split_blocks(all_keys), split_blocks(all_values))
    )
    own_keys, own_values = (
        lax.psum_scatter(
            key_parts[0].reshape(key_count, model_width).astype(jnp.bfloat16),
            "inner",
            scatter_dimension=0,
            tiled=True,
        ).astype(jnp.float32),
        lax.psum_scatter(
            key_parts[1].reshape(key_count, model_width).astype(jnp.bfloat16),
            "inner",
            scatter_dimension=0,
            tiled=True,
        ).astype(jnp.float32),
    )
    split_value, pull_split = jax.vjp(split_heads, projected)
    grad_projected = pull_split(
        (
            grad_query,
            own_keys.reshape(row_count, head_count, HEAD_DIM),
            own_values.reshape(row_count, head_count, HEAD_DIM),
        )
    )[0].astype(jnp.bfloat16)
    grad_qkv = contract_rows(normed_one, grad_projected)
    grad_normed_one = contract_cols(grad_projected, w_qkv)
    first_value, pull_one = jax.vjp(norm_rows, inputs, gain_first)
    back_inputs, grad_gain_one = pull_one(grad_normed_one)
    input_grad = (grad_middle + back_inputs).astype(jnp.bfloat16)
    summed = (
        lax.psum_scatter(
            grad_qkv.astype(jnp.bfloat16), "inner", scatter_dimension=0, tiled=True
        ).astype(jnp.float32),
        lax.psum_scatter(
            grad_wout.astype(jnp.bfloat16), "inner", scatter_dimension=0, tiled=True
        ).astype(jnp.float32),
        lax.psum_scatter(
            grad_in.astype(jnp.bfloat16), "inner", scatter_dimension=0, tiled=True
        ).astype(jnp.float32),
        lax.psum_scatter(
            grad_down.astype(jnp.bfloat16), "inner", scatter_dimension=0, tiled=True
        ).astype(jnp.float32),
        lax.psum_scatter(
            grad_gain_one.astype(jnp.bfloat16), "inner", scatter_dimension=0, tiled=True
        ).astype(jnp.float32),
        lax.psum_scatter(
            grad_gain_two.astype(jnp.bfloat16), "inner", scatter_dimension=0, tiled=True
        ).astype(jnp.float32),
    )
    summed = (
        lax.psum(summed[0].astype(jnp.bfloat16), "rep").astype(jnp.float32),
        lax.psum(summed[1].astype(jnp.bfloat16), "rep").astype(jnp.float32),
        lax.psum(summed[2].astype(jnp.bfloat16), "rep").astype(jnp.float32),
        lax.psum(summed[3].astype(jnp.bfloat16), "rep").astype(jnp.float32),
        lax.psum(summed[4].astype(jnp.bfloat16), "rep").astype(jnp.float32),
        lax.psum(summed[5].astype(jnp.bfloat16), "rep").astype(jnp.float32),
    )
    return (
        layer_out.astype(jnp.bfloat16),
        input_grad,
        summed[0],
        summed[1],
        summed[2],
        summed[3],
        summed[4],
        summed[5],
    )


def solution(mesh):
    return jax.shard_map(
        on_device,
        mesh=mesh,
        in_specs=(
            P(("rep", "inner"), None),
            P(("rep", "inner"), None),
            P("inner", None),
            P("inner", None),
            P("inner", None),
            P("inner", None),
            P("inner"),
            P("inner"),
        ),
        out_specs=(
            P(("rep", "inner"), None),
            P(("rep", "inner"), None),
            P("inner", None),
            P("inner", None),
            P("inner", None),
            P("inner", None),
            P("inner"),
            P("inner"),
        ),
        check_vma=False,
    )
```

profile of v0, /device:TPU:0, one launch (start us, length us, event | category | flops | bytes accessed | tf_op | source)
XLA Modules:
  0.0 841.6 jit_solution(2752431351207426690)
XLA Ops:
  8.0 13.5 %all-gather = bf16[8,1,128]{2,1,0:T(2,128)(2,1)S(1)} all-gather(bf16[1,1,128]{2,1,0:T(2,128)(2,1)} %bitcast.152), channel_id=1, replica_groups=mesh['rep'=4,'inner'=8] {'inner'}, dimensions={0}, use_global_device_ids=true | all-gather | bytes 2304 | tf_op jit(solution)/shard_map/all_gather | solution.py:59
  24.0 53.2 %all-gather.9.cloned.1.call-done = bf16[1024,3072]{1,0:T(8,128)(2,1)} async-done(((bf16[128,3072]{1,0:T(8,128)(2,1)}), bf16[1024,3072]{1,0:T(8,128)(2,1)}) %all-gather.9.cloned.1.call-update) | async-done | bytes 6291472 | tf_op jit(solution)/shard_map/all_gather | solution.py:55
  85.1 9.2 %all-gather.1 = bf16[8,1,128]{2,1,0:T(2,128)(2,1)S(1)} all-gather(bf16[1,1,128]{2,1,0:T(2,128)(2,1)S(1)} %bitcast.153), channel_id=1, replica_groups=mesh['rep'=4,'inner'=8] {'inner'}, dimensions={0}, use_global_device_ids=true | all-gather | bytes 2304 | tf_op jit(solution)/shard_map/all_gather | solution.py:60
  94.3 17.8 %all-gather.13.cloned.1.call-done = bf16[1024,1024]{0,1:T(8,128)(2,1)} async-done(((bf16[128,1024]{0,1:T(8,128)(2,1)}), bf16[1024,1024]{0,1:T(8,128)(2,1)}) %all-gather.13.cloned.1.call-update) | async-done | bytes 2097168 | tf_op jit(solution)/shard_map/all_gather | solution.py:95
  112.1 4.5 reshape.175
  118.6 23.9 %all-gather.11.cloned.1.call-done = bf16[1024,1024]{1,0:T(8,128)(2,1)} async-done(((bf16[128,1024]{1,0:T(8,128)(2,1)}), bf16[1024,1024]{1,0:T(8,128)(2,1)}) %all-gather.11.cloned.1.call-update) | async-done | bytes 2097168 | tf_op jit(solution)/shard_map/all_gather | solution.py:96
  142.5 6.4 reshape.196
  148.8 5.5 copy.46
  154.4 11.6 %while.39 = (s32[]{:T(128)}, f32[16,128]{1,0:T(8,128)S(1)}, f32[16,128]{1,0:T(8,128)S(1)}, bf16[2,512,16,64]{1,3,2,0:T(8,128)(2,1)S(1)}, bf16[128,16,64]{0,2,1:T(8,128)(2,1)S(1)}, /*index=5*/s32[]{:T(128)}, s32[]{:T(128)}) while((s32[]{:T(128)}, f32[16,128]{1,0:T(8,128)S(1)}, f32[16,128]{1,0:T(8,128)S(1)}, ...), condition=%wide.region_5.6_spmd.clone, body=%wide.region_2.5_spmd.clone.sunk | while | flops 139470848 | bytes 9805916 | solution.py:122
  165.9 6.0 while.40
  175.1 100.1 %all-gather.17.cloned.1.call-done = bf16[1024,5248]{1,0:T(8,128)(2,1)} async-done(((bf16[128,5248]{1,0:T(8,128)(2,1)}), bf16[1024,5248]{1,0:T(8,128)(2,1)}) %all-gather.17.cloned.1.call-update) | async-done | bytes 10747920 | tf_op jit(solution)/shard_map/all_gather | solution.py:57
  275.1 7.3 fusion.73
  282.4 49.7 %all-gather.19.cloned.1.call-done = bf16[2624,1024]{1,0:T(8,128)(2,1)} async-done(((bf16[328,1024]{1,0:T(8,128)(2,1)}), bf16[2624,1024]{1,0:T(8,128)(2,1)}) %all-gather.19.cloned.1.call-update) | async-done | bytes 5373968 | tf_op jit(solution)/shard_map/all_gather | solution.py:58
  332.1 7.0 fusion.57
  340.8 4.4 multiply_reduce_fusion
  352.1 21.2 %while.41 = (s32[]{:T(128)}, f32[128,16,64]{0,2,1:T(8,128)}, bf16[2,512,16,64]{1,3,2,0:T(8,128)(2,1)}, bf16[2,512,16,64]{1,3,2,0:T(8,128)(2,1)}, bf16[2,512,16,6...) while((s32[]{:T(128)}, f32[128,16,64]{0,2,1:T(8,128)}, ...), condition=%wide.region_14.15_spmd.clone, body=%wide.region_13.14_spmd.clone.sunk | while | flops 680394752 | bytes 87058192 | solution.py:207
  373.3 6.2 copy.63
  379.5 6.5 reshape.192
  387.6 4.8 copy.62
  392.3 6.5 reshape.190
  407.3 13.4 %reduce-scatter.21.cloned.1.call-done = bf16[128,1024]{1,0:T(8,128)(2,1)} async-done(((bf16[1024,1024]{1,0:T(8,128)(2,1)}), bf16[128,1024]{1,0:T(8,128)(2,1)}) %reduce-scatter.21.cloned.1.call-update) | async-done | bytes 262160
  421.9 35.8 %reduce-scatter.19.cloned.1.call-done = bf16[128,1024]{1,0:T(8,128)(2,1)} async-done(((bf16[1024,1024]{1,0:T(8,128)(2,1)}), bf16[128,1024]{1,0:T(8,128)(2,1)}) %reduce-scatter.19.cloned.1.call-update) | async-done | bytes 262160
  459.1 4.6 convolution_convert_fusion.2
  465.1 7.3 convolution_convert_fusion
  472.5 21.9 %reduce-scatter.13.cloned.1.call-done = bf16[128,1024]{1,0:T(8,128)(2,1)} async-done(((bf16[1024,1024]{1,0:T(8,128)(2,1)}), bf16[128,1024]{1,0:T(8,128)(2,1)}) %reduce-scatter.13.cloned.1.call-update) | async-done | bytes 262160 | tf_op jit(solution)/shard_map/reduce_scatter | solution.py:241
  494.3 62.0 %reduce-scatter.17.cloned.1.call-done = bf16[328,1024]{1,0:T(8,128)(2,1)} async-done(((bf16[2624,1024]{1,0:T(8,128)(2,1)}), bf16[328,1024]{1,0:T(8,128)(2,1)}) %reduce-scatter.17.cloned.1.call-update) | async-done | bytes 671760 | tf_op jit(solution)/shard_map/reduce_scatter | solution.py:247
  556.3 70.6 %reduce-scatter.11.cloned.1.call-done = bf16[128,3072]{1,0:T(8,128)(2,1)} async-done(((bf16[1024,3072]{1,0:T(8,128)(2,1)}), bf16[128,3072]{1,0:T(8,128)(2,1)}) %reduce-scatter.11.cloned.1.call-update) | async-done | bytes 786448 | tf_op jit(solution)/shard_map/reduce_scatter | solution.py:238
  627.0 112.6 %reduce-scatter.15.cloned.1.call-done = bf16[128,5248]{1,0:T(8,128)(2,1)} async-done(((bf16[1024,5248]{1,0:T(8,128)(2,1)}), bf16[128,5248]{1,0:T(8,128)(2,1)}) %reduce-scatter.15.cloned.1.call-update) | async-done | bytes 1343504 | tf_op jit(solution)/shard_map/reduce_scatter | solution.py:244
  745.1 5.7 fusion.56
  751.2 13.6 %all-reduce.11 = (bf16[1024]{0:T(1024)(128)(2,1)S(1)}, bf16[1024]{0:T(1024)(128)(2,1)S(1)}) all-reduce(bf16[1024]{0:T(1024)(128)(2,1)S(1)} %get-tuple-element.260, bf16[1024]{0:T(1024)(128)(2,1)S(1)} %get-tuple-element.258), channel_id=8, replica_groups=mesh['rep'=4,'inner'=8] {'inner'}, use_global_device_ids=true, to_apply=%region_28.29.clone | all-reduce | flops 2048 | bytes 8192
  764.9 9.5 %all-reduce.12 = (bf16[128]{0:T(256)(128)(2,1)S(1)}, bf16[128]{0:T(256)(128)(2,1)S(1)}) all-reduce(bf16[128]{0:T(256)(128)(2,1)S(1)} %dynamic-slice.1, bf16[128]{0:T(256)(128)(2,1)S(1)} %dynamic-slice.3), channel_id=1, replica_groups=mesh['rep'=4,'inner'=8] {'rep'}, use_global_device_ids=true, to_apply=%region_29.30 | all-reduce | flops 256 | bytes 1024 | tf_op jit(solution)/shard_map/psum | solution.py:262
  776.4 52.0 %all-reduce.16.cloned.1.call-done = (bf16[128,3072]{1,0:T(8,128)(2,1)}, bf16[128,1024]{1,0:T(8,128)(2,1)}, bf16[128,5248]{1,0:T(8,128)(2,1)}, bf16[328,1024]{1,0:T(8,128)(2,1)}) async-done(((bf16[128,3072]{1,0:T(8,128)(2,1)}, bf16[128,1024]{1,0:T(8,128)(2,1)}, bf16[128,5248]{1,0:T(8,128)(2,1)}, bf16[328,1024]{1,0:T(8,128)(2,1)}), (bf16[128,3072]{1,0:T(8,128)(2,1)}, bf16[128,1024]{1,0:T(8,128)(2,1)}, ...) | async-done | bytes 3063824 | tf_op jit(solution)/shard_map/psum | solution.py:258
  (184 shorter events, 90.4 us)
Async XLA Ops:
  7.2 70.0 %copy-start.7 = (bf16[128,1024]{1,0:T(8,128)(2,1)S(1)}, bf16[128,1024]{1,0:T(8,128)(2,1)}, u32[]{:S(2)}) copy-start(bf16[128,1024]{1,0:T(8,128)(2,1)} %param.14) | copy-start | bytes 786436
  7.2 70.0 %all-gather.9.cloned.1.call-start = ((), (), s32[]{:S(2)}) async-start(), calls=%async_computation.6 | async-start | bytes 7077888 | tf_op jit(solution)/shard_map/all_gather | solution.py:55
  7.9 104.2 %all-gather.13.cloned.1.call-start = ((), (), s32[]{:S(2)}) async-start(), calls=%async_computation.8 | async-start | bytes 2359296 | tf_op jit(solution)/shard_map/all_gather | solution.py:95
  82.4 2.7 copy-start.31
  82.4 60.0 %all-gather.11.cloned.1.call-start = ((), (), s32[]{:S(2)}) async-start(), calls=%async_computation.7 | async-start | bytes 2359296 | tf_op jit(solution)/shard_map/all_gather | solution.py:96
  83.3 89.3 %all-gather.15.cloned.1.call-start = ((), (), s32[]{:S(2)}) async-start(), calls=%async_computation.9 | async-start | bytes 2359296 | tf_op jit(solution)/shard_map/all_gather | solution.py:56
  83.8 191.3 %all-gather.17.cloned.1.call-start = ((), (), s32[]{:S(2)}) async-start(), calls=%async_computation.10 | async-start | bytes 12091392 | tf_op jit(solution)/shard_map/all_gather | solution.py:57
  84.4 247.7 %all-gather.19.cloned.1.call-start = ((), (), s32[]{:S(2)}) async-start(), calls=%async_computation.11 | async-start | bytes 6045696 | tf_op jit(solution)/shard_map/all_gather | solution.py:58
  85.0 335.7 %reduce-scatter.21.cloned.1.call-start = ((), (), s32[]{:S(2)}) async-start(), calls=%async_computation.17 | async-start | bytes 2359296
  172.0 2.9 copy-start.20
  275.1 57.0 %copy-start.16 = (bf16[128,1024]{1,0:T(8,128)(2,1)S(1)}, bf16[128,1024]{1,0:T(8,128)(2,1)}, u32[]{:S(2)}) copy-start(bf16[128,1024]{1,0:T(8,128)(2,1)} %param.15) | copy-start | bytes 786436
  332.1 7.0 copy-start.10
  332.1 8.7 %copy-start.4 = (bf16[1024,5248]{1,0:T(8,128)(2,1)S(1)}, bf16[1024,5248]{1,0:T(8,128)(2,1)}, u32[]{:S(2)}) copy-start(bf16[1024,5248]{1,0:T(8,128)(2,1)} %all-gather.17.cloned.1.call-done) | copy-start | bytes 32243716
  340.8 4.4 copy-start.8
  345.2 3.1 copy-start.12
  353.6 2.6 copy-start
  358.1 2.7 copy-start.1
  368.5 2.8 copy-start.1
  386.0 71.6 %reduce-scatter.19.cloned.1.call-start = ((), (), s32[]{:S(2)}) async-start(), calls=%async_computation.16 | async-start | bytes 2359296
  398.9 95.4 %reduce-scatter.13.cloned.1.call-start = ((), (), s32[]{:S(2)}) async-start(), calls=%async_computation.13 | async-start | bytes 2359296 | tf_op jit(solution)/shard_map/reduce_scatter | solution.py:241
  402.0 154.4 %reduce-scatter.17.cloned.1.call-start = ((), (), s32[]{:S(2)}) async-start(), calls=%async_computation.15 | async-start | bytes 6045696 | tf_op jit(solution)/shard_map/reduce_scatter | solution.py:247
  407.0 51.8 %copy-start.6 = (f32[128,16,64]{0,2,1:T(8,128)S(1)}, f32[128,16,64]{0,2,1:T(8,128)}, u32[]{:S(2)}) copy-start(f32[128,16,64]{0,2,1:T(8,128)} %get-tuple-element.127) | copy-start | bytes 1572868
  407.0 219.9 %reduce-scatter.11.cloned.1.call-start = ((), (), s32[]{:S(2)}) async-start(), calls=%async_computation.12 | async-start | bytes 7077888 | tf_op jit(solution)/shard_map/reduce_scatter | solution.py:238
  459.0 4.6 copy-start.24
  459.1 4.6 copy-start.26
  463.7 275.8 %reduce-scatter.15.cloned.1.call-start = ((), (), s32[]{:S(2)}) async-start(), calls=%async_computation.14 | async-start | bytes 12091392 | tf_op jit(solution)/shard_map/reduce_scatter | solution.py:244
  472.4 267.2 %copy-start.32 = (u32[32]{0:T(128)S(1)}, u32[32]{0:T(128)}, u32[]{:S(2)}) copy-start(u32[32]{0:T(128)} %constant.153) | copy-start | bytes 388
  472.4 356.0 %all-reduce.16.cloned.1.call-start = ((), (), s32[]{:S(2)}) async-start(), calls=%async_computation.18 | async-start | bytes 6127616 | tf_op jit(solution)/shard_map/psum | solution.py:258
  740.8 4.3 copy-start.25
  740.8 4.3 copy-start.27
  745.1 30.3 %copy-start.15 = (f32[128,1024]{1,0:T(8,128)S(1)}, f32[128,1024]{1,0:T(8,128)}, u32[]{:S(2)}) copy-start(f32[128,1024]{1,0:T(8,128)} %copy-done.14) | copy-start | bytes 1572868
  828.4 3.1 copy-start.28
  (19 other events, 27.9 us)
Sparse Core Ops, SparseCore 0:
  9.7 67.4 all-gather.8
  82.5 29.4 all-gather.12
  114.3 28.1 all-gather.10
  143.9 28.5 all-gather.14
  174.0 101.0 all-gather.16
  276.6 55.4 all-gather.18
  386.1 34.5 reduce-scatter.20
  423.0 34.6 reduce-scatter.18
  460.0 34.3 reduce-scatter.12
  496.5 59.8 reduce-scatter.16
  558.7 68.1 reduce-scatter.10
  629.2 110.2 reduce-scatter.14
  743.5 84.9 all-reduce.15
where the time goes:
time: 849 us; the launch traced here: 842 us
  waiting for transfers between devices  616 us (73%)
  matrix products  82.5 us (10%)
  local copies, waits for them, and re-layouts  57.8 us (7%)
  blocking collectives  45.8 us (5%)
  other arithmetic  23 us (3%)
  between operations  15.2 us (2%)
    reduce_scatter x1, waiting for transfers between devices, on_device(): lax.psum_scatter(grad_in.astype(jnp.bfloat16), 'inner', scatter_dimension...  113 us
    all_gather x1, waiting for transfers between devices, on_device(): lax.all_gather(in_weight, 'inner', axis=0, tiled=True)  100 us
    reduce_scatter x1, waiting for transfers between devices, on_device(): lax.psum_scatter(grad_qkv.astype(jnp.bfloat16), 'inner', scatter_dimensio...  70.6 us
    reduce_scatter x1, waiting for transfers between devices, on_device(): lax.psum_scatter(grad_down.astype(jnp.bfloat16), 'inner', scatter_dimensi...  62 us
    all_gather x1, waiting for transfers between devices, on_device(): lax.all_gather(qkv_weight, 'inner', axis=0, tiled=True)  53.2 us
    psum x1, waiting for transfers between devices, on_device(): lax.psum(summed[0].astype(jnp.bfloat16), 'rep').astype(jnp.float32)  52 us
    unnamed x15, waiting for transfers between devices  51.6 us
    all_gather x1, waiting for transfers between devices, on_device(): lax.all_gather(down_weight, 'inner', axis=0, tiled=True)  49.7 us
  transfers between devices with their start and end apart: 13, of which 13 were waited for; matrix products, arithmetic and copies ran while one was open for 11% of the time, Pallas kernels for 0%

commit v1 on v0

--- a/solution.py
+++ b/solution.py
@@ -255,7 +255,9 @@
         ).astype(jnp.float32),
     )
     summed = (
-        lax.psum(summed[0].astype(jnp.bfloat16), "rep").astype(jnp.float32),
+        lax.all_gather(summed[0].astype(jnp.bfloat16), axis_name="rep")
+        .sum(axis=0)
+        .astype(jnp.float32),
         lax.psum(summed[1].astype(jnp.bfloat16), "rep").astype(jnp.float32),
         lax.psum(summed[2].astype(jnp.bfloat16), "rep").astype(jnp.float32),
         lax.psum(summed[3].astype(jnp.bfloat16), "rep").astype(jnp.float32),

time: 849 us -> 884 us (1.041)
  waiting for transfers between devices: 616 us -> 648 us
    psum x1, waiting for transfers between devices: 52 us -> 72.8 us  [on_device(): lax.psum(summed[1].astype(jnp.bfloat16), 'rep').astype(jnp.float32)]
    reduce_scatter x1, waiting for transfers between devices: 70.6 us -> 51.8 us  [on_device(): lax.psum_scatter(grad_qkv.astype(jnp.bfloat16), 'inner', scatter_dimensio...]
    reduce_scatter x1, waiting for transfers between devices: 21.9 us -> 36.8 us  [on_device(): lax.psum_scatter(grad_wout.astype(jnp.bfloat16), 'inner', scatter_dimensi...]
    unnamed x15 -> x16, waiting for transfers between devices: 51.6 us -> 59.6 us
    unnamed x67 -> x65, local copies, waits for them, and re-layouts: 41.2 us -> 40.8 us
  transfers between devices with their start and end apart: 13 -> 14, of which waited for: 13 -> 14; matrix products, arithmetic and copies ran while one was open for 11% -> 10% of each run, Pallas kernels for 0% -> 0%
where the time goes in v1:
time: 884 us; the launch traced here: 877 us
  waiting for transfers between devices  648 us (73%)
  matrix products  82.5 us (9%)
  local copies, waits for them, and re-layouts  57.5 us (7%)
  blocking collectives  46.3 us (5%)
  other arithmetic  25.5 us (3%)
  between operations  15.2 us (2%)
    reduce_scatter x1, waiting for transfers between devices, on_device(): lax.psum_scatter(grad_in.astype(jnp.bfloat16), 'inner', scatter_dimension...  113 us
    all_gather x1, waiting for transfers between devices, on_device(): lax.all_gather(in_weight, 'inner', axis=0, tiled=True)  100 us
    psum x1, waiting for transfers between devices, on_device(): lax.psum(summed[1].astype(jnp.bfloat16), 'rep').astype(jnp.float32)  72.8 us
    reduce_scatter x1, waiting for transfers between devices, on_device(): lax.psum_scatter(grad_down.astype(jnp.bfloat16), 'inner', scatter_dimensi...  62.1 us
    unnamed x16, waiting for transfers between devices  59.6 us
    all_gather x1, waiting for transfers between devices, on_device(): lax.all_gather(qkv_weight, 'inner', axis=0, tiled=True)  53.2 us
    reduce_scatter x1, waiting for transfers between devices, on_device(): lax.psum_scatter(grad_qkv.astype(jnp.bfloat16), 'inner', scatter_dimensio...  51.8 us
    all_gather x1, waiting for transfers between devices, on_device(): lax.all_gather(down_weight, 'inner', axis=0, tiled=True)  49.7 us
  transfers between devices with their start and end apart: 14, of which 14 were waited for; matrix products, arithmetic and copies ran while one was open for 10% of the time, Pallas kernels for 0%

profile of v1, /device:TPU:0, one launch (start us, length us, event | category | flops | bytes accessed | tf_op | source)
XLA Modules:
  0.0 876.8 jit_solution(4694918390599267419)
XLA Ops:
  8.0 13.5 %all-gather.1 = bf16[8,1,128]{2,1,0:T(2,128)(2,1)S(1)} all-gather(bf16[1,1,128]{2,1,0:T(2,128)(2,1)} %bitcast.154), channel_id=1, replica_groups=mesh['rep'=4,'inner'=8] {'inner'}, dimensions={0}, use_global_device_ids=true | all-gather | bytes 2304 | tf_op jit(solution)/shard_map/all_gather | solution.py:59
  24.0 53.2 %all-gather.11.cloned.1.call-done = bf16[1024,3072]{1,0:T(8,128)(2,1)} async-done(((bf16[128,3072]{1,0:T(8,128)(2,1)}), bf16[1024,3072]{1,0:T(8,128)(2,1)}) %all-gather.11.cloned.1.call-update) | async-done | bytes 6291472 | tf_op jit(solution)/shard_map/all_gather | solution.py:55
  85.1 9.2 %all-gather.2 = bf16[8,1,128]{2,1,0:T(2,128)(2,1)S(1)} all-gather(bf16[1,1,128]{2,1,0:T(2,128)(2,1)S(1)} %bitcast.155), channel_id=1, replica_groups=mesh['rep'=4,'inner'=8] {'inner'}, dimensions={0}, use_global_device_ids=true | all-gather | bytes 2304 | tf_op jit(solution)/shard_map/all_gather | solution.py:60
  94.3 17.8 %all-gather.15.cloned.1.call-done = bf16[1024,1024]{0,1:T(8,128)(2,1)} async-done(((bf16[128,1024]{0,1:T(8,128)(2,1)}), bf16[1024,1024]{0,1:T(8,128)(2,1)}) %all-gather.15.cloned.1.call-update) | async-done | bytes 2097168 | tf_op jit(solution)/shard_map/all_gather | solution.py:95
  112.1 4.5 reshape.175
  118.6 23.9 %all-gather.13.cloned.1.call-done = bf16[1024,1024]{1,0:T(8,128)(2,1)} async-done(((bf16[128,1024]{1,0:T(8,128)(2,1)}), bf16[1024,1024]{1,0:T(8,128)(2,1)}) %all-gather.13.cloned.1.call-update) | async-done | bytes 2097168 | tf_op jit(solution)/shard_map/all_gather | solution.py:96
  142.5 6.4 reshape.197
  148.9 5.5 copy.46
  154.3 11.6 %while.39 = (s32[]{:T(128)}, f32[16,128]{1,0:T(8,128)S(1)}, f32[16,128]{1,0:T(8,128)S(1)}, bf16[2,512,16,64]{1,3,2,0:T(8,128)(2,1)S(1)}, bf16[128,16,64]{0,2,1:T(8,128)(2,1)S(1)}, /*index=5*/s32[]{:T(128)}, s32[]{:T(128)}) while((s32[]{:T(128)}, f32[16,128]{1,0:T(8,128)S(1)}, f32[16,128]{1,0:T(8,128)S(1)}, ...), condition=%wide.region_5.6_spmd.clone, body=%wide.region_2.5_spmd.clone.sunk | while | flops 139470848 | bytes 9805916 | solution.py:122
  166.0 6.0 while.40
  175.1 100.0 %all-gather.19.cloned.1.call-done = bf16[1024,5248]{1,0:T(8,128)(2,1)} async-done(((bf16[128,5248]{1,0:T(8,128)(2,1)}), bf16[1024,5248]{1,0:T(8,128)(2,1)}) %all-gather.19.cloned.1.call-update) | async-done | bytes 10747920 | tf_op jit(solution)/shard_map/all_gather | solution.py:57
  275.1 7.3 fusion.73
  282.4 49.7 %all-gather.21.cloned.1.call-done = bf16[2624,1024]{1,0:T(8,128)(2,1)} async-done(((bf16[328,1024]{1,0:T(8,128)(2,1)}), bf16[2624,1024]{1,0:T(8,128)(2,1)}) %all-gather.21.cloned.1.call-update) | async-done | bytes 5373968 | tf_op jit(solution)/shard_map/all_gather | solution.py:58
  332.1 7.0 fusion.57
  352.1 21.2 %while.41 = (s32[]{:T(128)}, f32[128,16,64]{0,2,1:T(8,128)}, bf16[2,512,16,64]{1,3,2,0:T(8,128)(2,1)}, bf16[2,512,16,64]{1,3,2,0:T(8,128)(2,1)}, bf16[2,512,16,6...) while((s32[]{:T(128)}, f32[128,16,64]{0,2,1:T(8,128)}, ...), condition=%wide.region_14.15_spmd.clone, body=%wide.region_13.14_spmd.clone.sunk | while | flops 680394752 | bytes 87058192 | solution.py:207
  373.2 6.2 copy.63
  379.5 6.5 reshape.193
  387.5 4.8 copy.62
  392.3 6.5 reshape.191
  398.9 21.8 %reduce-scatter.21.cloned.1.call-done = bf16[128,1024]{1,0:T(8,128)(2,1)} async-done(((bf16[1024,1024]{1,0:T(8,128)(2,1)}), bf16[128,1024]{1,0:T(8,128)(2,1)}) %reduce-scatter.21.cloned.1.call-update) | async-done | bytes 262160
  422.2 35.3 %reduce-scatter.19.cloned.1.call-done = bf16[128,1024]{1,0:T(8,128)(2,1)} async-done(((bf16[1024,1024]{1,0:T(8,128)(2,1)}), bf16[128,1024]{1,0:T(8,128)(2,1)}) %reduce-scatter.19.cloned.1.call-update) | async-done | bytes 262160
  458.6 4.6 convolution_convert_fusion.2
  472.8 7.3 convolution_convert_fusion
  480.1 51.8 %reduce-scatter.11.cloned.1.call-done = bf16[128,3072]{1,0:T(8,128)(2,1)} async-done(((bf16[1024,3072]{1,0:T(8,128)(2,1)}), bf16[128,3072]{1,0:T(8,128)(2,1)}) %reduce-scatter.11.cloned.1.call-update) | async-done | bytes 786448 | tf_op jit(solution)/shard_map/reduce_scatter | solution.py:238
  532.0 36.8 %reduce-scatter.13.cloned.1.call-done = bf16[128,1024]{1,0:T(8,128)(2,1)} async-done(((bf16[1024,1024]{1,0:T(8,128)(2,1)}), bf16[128,1024]{1,0:T(8,128)(2,1)}) %reduce-scatter.13.cloned.1.call-update) | async-done | bytes 262160 | tf_op jit(solution)/shard_map/reduce_scatter | solution.py:241
  568.9 62.1 %reduce-scatter.17.cloned.1.call-done = bf16[328,1024]{1,0:T(8,128)(2,1)} async-done(((bf16[2624,1024]{1,0:T(8,128)(2,1)}), bf16[328,1024]{1,0:T(8,128)(2,1)}) %reduce-scatter.17.cloned.1.call-update) | async-done | bytes 671760 | tf_op jit(solution)/shard_map/reduce_scatter | solution.py:247
  631.0 112.6 %reduce-scatter.15.cloned.1.call-done = bf16[128,5248]{1,0:T(8,128)(2,1)} async-done(((bf16[1024,5248]{1,0:T(8,128)(2,1)}), bf16[128,5248]{1,0:T(8,128)(2,1)}) %reduce-scatter.15.cloned.1.call-update) | async-done | bytes 1343504 | tf_op jit(solution)/shard_map/reduce_scatter | solution.py:244
  749.1 5.7 fusion.56
  755.1 13.6 %all-reduce.11 = (bf16[1024]{0:T(1024)(128)(2,1)S(1)}, bf16[1024]{0:T(1024)(128)(2,1)S(1)}) all-reduce(bf16[1024]{0:T(1024)(128)(2,1)S(1)} %get-tuple-element.260, bf16[1024]{0:T(1024)(128)(2,1)S(1)} %get-tuple-element.258), channel_id=9, replica_groups=mesh['rep'=4,'inner'=8] {'inner'}, use_global_device_ids=true, to_apply=%region_28.29.clone | all-reduce | flops 2048 | bytes 8192
  768.9 10.0 %all-reduce.12 = (bf16[128]{0:T(256)(128)(2,1)S(1)}, bf16[128]{0:T(256)(128)(2,1)S(1)}) all-reduce(bf16[128]{0:T(256)(128)(2,1)S(1)} %dynamic-slice.1, bf16[128]{0:T(256)(128)(2,1)S(1)} %dynamic-slice.3), channel_id=1, replica_groups=mesh['rep'=4,'inner'=8] {'rep'}, use_global_device_ids=true, to_apply=%region_29.30 | all-reduce | flops 256 | bytes 1024 | tf_op jit(solution)/shard_map/psum | solution.py:264
  780.9 7.3 all-gather.23.cloned.1.call-done
  792.0 72.8 %all-reduce.16.cloned.1.call-done = (bf16[128,1024]{1,0:T(8,128)(2,1)}, bf16[128,5248]{1,0:T(8,128)(2,1)}, bf16[328,1024]{1,0:T(8,128)(2,1)}) async-done(((bf16[128,1024]{1,0:T(8,128)(2,1)}, bf16[128,5248]{1,0:T(8,128)(2,1)}, bf16[328,1024]{1,0:T(8,128)(2,1)}), (bf16[128,1024]{1,0:T(8,128)(2,1)}, bf16[128,5248]{1,0:T(8,128)(2,1)}, bf16[328,1024]{1,0:T(8,128)(2,1)})) %all-reduce.16.cloned.1.call-update) | async-done | bytes 2277392 | tf_op jit(solution)/shard_map/psum | solution.py:261
  (186 shorter events, 97.1 us)
Async XLA Ops:
  7.2 70.0 %copy-start.7 = (bf16[128,1024]{1,0:T(8,128)(2,1)S(1)}, bf16[128,1024]{1,0:T(8,128)(2,1)}, u32[]{:S(2)}) copy-start(bf16[128,1024]{1,0:T(8,128)(2,1)} %param.14) | copy-start | bytes 786436
  7.2 70.0 %all-gather.11.cloned.1.call-start = ((), (), s32[]{:S(2)}) async-start(), calls=%async_computation.6 | async-start | bytes 7077888 | tf_op jit(solution)/shard_map/all_gather | solution.py:55
  7.9 104.2 %all-gather.15.cloned.1.call-start = ((), (), s32[]{:S(2)}) async-start(), calls=%async_computation.8 | async-start | bytes 2359296 | tf_op jit(solution)/shard_map/all_gather | solution.py:95
  82.4 2.7 copy-start.30
  82.4 60.0 %all-gather.13.cloned.1.call-start = ((), (), s32[]{:S(2)}) async-start(), calls=%async_computation.7 | async-start | bytes 2359296 | tf_op jit(solution)/shard_map/all_gather | solution.py:96
  83.3 89.3 %all-gather.17.cloned.1.call-start = ((), (), s32[]{:S(2)}) async-start(), calls=%async_computation.9 | async-start | bytes 2359296 | tf_op jit(solution)/shard_map/all_gather | solution.py:56
  83.8 191.3 %all-gather.19.cloned.1.call-start = ((), (), s32[]{:S(2)}) async-start(), calls=%async_computation.10 | async-start | bytes 12091392 | tf_op jit(solution)/shard_map/all_gather | solution.py:57
  84.4 247.7 %all-gather.21.cloned.1.call-start = ((), (), s32[]{:S(2)}) async-start(), calls=%async_computation.11 | async-start | bytes 6045696 | tf_op jit(solution)/shard_map/all_gather | solution.py:58
  85.0 335.7 %reduce-scatter.21.cloned.1.call-start = ((), (), s32[]{:S(2)}) async-start(), calls=%async_computation.18 | async-start | bytes 2359296
  172.0 2.9 copy-start.20
  275.1 57.0 %copy-start.16 = (bf16[128,1024]{1,0:T(8,128)(2,1)S(1)}, bf16[128,1024]{1,0:T(8,128)(2,1)}, u32[]{:S(2)}) copy-start(bf16[128,1024]{1,0:T(8,128)(2,1)} %param.15) | copy-start | bytes 786436
  332.1 7.0 copy-start.10
  332.1 8.7 copy-start.4
  340.8 4.4 copy-start.8
  345.2 3.1 copy-start.12
  358.0 2.7 copy-start.1
  368.4 2.8 copy-start.1
  386.0 71.5 %reduce-scatter.19.cloned.1.call-start = ((), (), s32[]{:S(2)}) async-start(), calls=%async_computation.17 | async-start | bytes 2359296
  398.8 23.1 %copy-start.6 = (f32[128,16,64]{0,2,1:T(8,128)S(1)}, f32[128,16,64]{0,2,1:T(8,128)}, u32[]{:S(2)}) copy-start(f32[128,16,64]{0,2,1:T(8,128)} %get-tuple-element.127) | copy-start | bytes 1572868
  398.8 133.1 %reduce-scatter.11.cloned.1.call-start = ((), (), s32[]{:S(2)}) async-start(), calls=%async_computation.12 | async-start | bytes 7077888 | tf_op jit(solution)/shard_map/reduce_scatter | solution.py:238
  422.1 41.1 %copy-start.24 = (f32[128,16,64]{0,2,1:T(8,128)}, f32[128,16,64]{0,2,1:T(8,128)S(1)}, u32[]{:S(2)}) copy-start(f32[128,16,64]{0,2,1:T(8,128)S(1)} %get-tuple-element.341) | copy-start | bytes 1572868
  422.2 41.1 %copy-start.26 = (f32[128,16,64]{0,2,1:T(8,128)}, f32[128,16,64]{0,2,1:T(8,128)S(1)}, u32[]{:S(2)}) copy-start(f32[128,16,64]{0,2,1:T(8,128)S(1)} %get-tuple-element.342) | copy-start | bytes 1572868
  463.3 105.6 %reduce-scatter.13.cloned.1.call-start = ((), (), s32[]{:S(2)}) async-start(), calls=%async_computation.13 | async-start | bytes 2359296 | tf_op jit(solution)/shard_map/reduce_scatter | solution.py:241
  466.3 164.7 %reduce-scatter.17.cloned.1.call-start = ((), (), s32[]{:S(2)}) async-start(), calls=%async_computation.15 | async-start | bytes 6045696 | tf_op jit(solution)/shard_map/reduce_scatter | solution.py:247
  471.5 272.1 %reduce-scatter.15.cloned.1.call-start = ((), (), s32[]{:S(2)}) async-start(), calls=%async_computation.14 | async-start | bytes 12091392 | tf_op jit(solution)/shard_map/reduce_scatter | solution.py:244
  480.1 263.5 %copy-start.31 = (u32[32]{0:T(128)S(1)}, u32[32]{0:T(128)}, u32[]{:S(2)}) copy-start(u32[32]{0:T(128)} %constant.154) | copy-start | bytes 388
  480.1 308.1 %all-gather.23.cloned.1.call-start = ((), (), s32[]{:S(2)}) async-start(), calls=%async_computation.16 | async-start | bytes 3932160 | tf_op jit(solution)/shard_map/all_gather | solution.py:258
  532.0 332.9 %all-reduce.16.cloned.1.call-start = ((), (), s32[]{:S(2)}) async-start(), calls=%async_computation.19 | async-start | bytes 4554752 | tf_op jit(solution)/shard_map/psum | solution.py:261
  744.8 4.3 copy-start.25
  744.8 4.2 copy-start.27
  749.1 30.8 %copy-start.15 = (f32[128,1024]{1,0:T(8,128)S(1)}, f32[128,1024]{1,0:T(8,128)}, u32[]{:S(2)}) copy-start(f32[128,1024]{1,0:T(8,128)} %copy-done.14) | copy-start | bytes 1572868
  864.8 3.1 copy-start.28
  (19 other events, 29.1 us)
Sparse Core Ops, SparseCore 0:
  9.7 67.4 all-gather.10
  82.5 29.4 all-gather.14
  114.3 28.1 all-gather.12
  143.9 28.5 all-gather.16
  174.0 101.0 all-gather.18
  276.6 55.4 all-gather.20
  386.1 34.5 reduce-scatter.20
  423.0 34.4 reduce-scatter.18
  463.4 68.5 reduce-scatter.10
  534.7 34.1 reduce-scatter.12
  571.2 59.7 reduce-scatter.16
  633.3 110.2 reduce-scatter.14
  745.5 42.5 all-gather.22
  791.9 72.9 all-reduce.15
